TPU v7x, 256 devices: a whole 4x4x8 slice. The times are simulated.
256 devices in a mesh: buoy: 4 (over x), dom: 64 (over z, y, core).
Axes of the slice: x: 4, y: 4, z: 8, core: 2. Of those that a mesh axis runs over, the one named last changes fastest.
Arguments:
- ambient: float32 [32, 36, 448], P('buoy', None, 'dom'), may hold values from -6 to 6
- initial_out: float32 [32, 36, 448], P('buoy', None, 'dom'), may hold values from -6 to 6
- translation: bfloat16 [512, 448, 448], P(('buoy', 'dom')), may hold values from -0.0625 to 0.0625
- pair_source: int32 [512], P(('buoy', 'dom')), may hold values from 0 to 31, as said below
- pair_target: int32 [512], P(('buoy', 'dom')), may hold values from 0 to 31, as said below
- pair_live: int32 [512], P(('buoy', 'dom')), may hold values from 0 to 1, as said below
- diffract: bfloat16 [448, 448], P('dom'), may hold values from -0.25 to 0.25
- panel_rows: bfloat16 [8192, 448], P('dom'), may hold values from -0.25 to 0.25
Outputs:
- outgoing: float32 [32, 36, 448], P('buoy', None, 'dom')
- sources: bfloat16 [32, 36, 8192], P('buoy', None, 'dom')
Inputs may be any that keep to these rules, and one draw needn't show every extreme that they name: `pair_target`: the slots of one device name target buoys among the 8 buoys of its index of buoy. `pair_source`: A source buoy differs from its target by 1 to 8 places in the farm's order; the live slots of one target name distinct sources. `pair_live`: A slot is live exactly where its source lies inside the farm; some device has all 2 live.
All inputs are finite; a program needn't handle non-finite values.
Results may differ from a plain program's by a relative error of at most 0.015.
Values may be sent and summed in bfloat16 or wider, within the bound.
No kernel may reach another device: no remote copies, remote signals or barrier semaphores. Data moves between devices by JAX's collectives and lax.ppermute only.
A program may use at most 64 MiB of HBM per device.

v0:
```python
import jax
import jax.numpy as jnp
from jax import lax
from jax.sharding import PartitionSpec as P

ITERS = 2


def extended_2(block, sides, width):
    for axis, dim in sides:
        count = lax.axis_size(axis)
        forward = [(i, i + 1) for i in range(count - 1)]
        backward = [(target, source) for source, target in forward]
        low = lax.ppermute(
            lax.slice_in_dim(block, block.shape[dim] - width, None, axis=dim), axis, forward
        )
        high = lax.ppermute(lax.slice_in_dim(block, 0, width, axis=dim), axis, backward)
        block = jnp.concatenate([low, block, high], axis=dim)
    return block


def rows_product(left, right):
    return lax.dot_general(
        left, right, (((1,), (1,)), ((), ())), preferred_element_type=jnp.float32
    )


def shards(
    ambient, initial_out, translation, pair_source, pair_target, pair_live, diffract, panel_rows
):
    per_dev, headings, share_width = initial_out.shape
    full_width = translation.shape[1]
    first_buoy = lax.axis_index("buoy") * per_dev
    column_start = lax.axis_index("dom") * share_width
    rows_source = pair_source - (first_buoy - per_dev)
    rows_target = pair_target - first_buoy
    place_table = (
        (rows_target[None, :] == jnp.arange(per_dev, dtype=jnp.int32)[:, None])
        & (pair_live[None, :] == 1)
    ).astype(jnp.float32)
    matrices = translation.astype(jnp.float32)
    coeffs = initial_out
    incident_bf = None
    for step in range(ITERS):
        whole = lax.all_gather(coeffs, "dom", axis=2, tiled=True)
        extended = extended_2(whole.astype(jnp.bfloat16), (("buoy", 0),), per_dev).astype(
            whole.dtype
        )
        picked = jnp.take(extended, rows_source, axis=0)
        terms = jnp.einsum("phn,pmn->phm", picked, matrices, precision=lax.Precision.HIGHEST)
        partial_value = jnp.einsum(
            "kp,phm->khm", place_table, terms, precision=lax.Precision.HIGHEST
        )
        own_columns = (
            lax.dynamic_slice_in_dim(partial_value, column_start, share_width, 2) + ambient
        )
        partial_value = lax.dynamic_update_slice_in_dim(partial_value, own_columns, column_start, 2)
        incident = lax.psum(partial_value, "dom")
        incident_bf = incident.astype(jnp.bfloat16)
        flat = incident_bf.reshape(per_dev * headings, full_width)
        coeffs = rows_product(flat, diffract).reshape(per_dev, headings, share_width)
    flat = incident_bf.reshape(per_dev * headings, full_width)
    sources = (
        rows_product(flat, panel_rows)
        .astype(jnp.bfloat16)
        .reshape(per_dev, headings, panel_rows.shape[0])
    )
    return (coeffs, sources)


def solution(mesh):
    in_specs = (
        P("buoy", None, "dom"),
        P("buoy", None, "dom"),
        P(("buoy", "dom"), None, None),
        P(("buoy", "dom")),
        P(("buoy", "dom")),
        P(("buoy", "dom")),
        P("dom", None),
        P("dom", None),
    )
    out_specs = (P("buoy", None, "dom"), P("buoy", None, "dom"))
    return jax.shard_map(shards, mesh=mesh, in_specs=in_specs, out_specs=out_specs, check_vma=False)
```

profile of v0, /device:TPU:6, one launch (start us, length us, event | category | flops | bytes accessed | tf_op | source)
XLA Modules:
  0.0 659.2 jit_solution(17983448239093237719)
XLA Ops:
  0.6 0.0 copy-start
  0.6 0.0 copy-start.6
  0.7 0.0 copy-start.4
  0.7 0.0 copy-start.3
  0.7 0.0 copy-start.7
  0.7 0.8 convert.2
  1.5 53.9 %all_gather.6 = bf16[8,36,448]{1,0,2:T(8,128)(2,1)S(1)} all-gather(bf16[8,36,7]{1,0,2:T(8,128)(2,1)S(1)} %convert.2), channel_id=1, replica_groups=mesh['buoy'=4,'dom'=64] {'dom'}, dimensions={2}, use_global_device_ids=true | all-gather | bytes 262080 | tf_op jit(solution)/shard_map/all_gather | solution.py:45
  55.4 0.7 copy.70
  56.1 2.7 collective-permute-start.1
  58.9 1.3 collective-permute-start
  60.2 0.0 copy-done.6
  60.2 0.0 copy-done.4
  60.2 0.0 copy-done.3
  60.3 0.2 copy.72
  60.4 0.0 copy-done.7
  60.4 5.9 collective-permute-done.1
  66.3 0.0 copy-start.1
  66.3 0.7 copy-done.1
  67.0 3.5 collective-permute-done
  70.6 1.3 maximum_convert_fusion
  71.8 0.6 gather_fusion
  72.4 0.0 copy-done
  72.4 0.0 copy-start.5
  72.4 0.9 fusion.4
  73.3 0.6 fusion.8
  73.9 0.1 dynamic-slice_add_fusion.1
  74.0 0.6 dynamic_update_slice.6
  74.6 258.2 %all-reduce.2 = bf16[8,36,448]{2,0,1:T(8,128)(2,1)S(1)} all-reduce(f32[8,36,448]{2,0,1:T(8,128)S(1)} %dynamic_update_slice.6), channel_id=1, replica_groups=mesh['buoy'=4,'dom'=64] {'dom'}, use_global_device_ids=true, to_apply=%region_0.0 | all-reduce | flops 129024 | bytes 774144 | tf_op jit(solution)/shard_map/psum | solution.py:58
  332.9 0.0 copy-done.5
  332.9 0.3 fusion
  333.2 47.3 %all_gather.7 = bf16[8,36,448]{1,0,2:T(8,128)(2,1)S(1)} all-gather(bf16[8,36,7]{1,0,2:T(8,128)(2,1)S(1)} %copy.74), channel_id=1, replica_groups=mesh['buoy'=4,'dom'=64] {'dom'}, dimensions={2}, use_global_device_ids=true | all-gather | bytes 262080 | tf_op jit(solution)/shard_map/all_gather | solution.py:45
  380.5 0.9 copy.75
  381.4 2.4 collective-permute-start.3
  383.9 1.5 collective-permute-start.2
  385.3 5.3 collective-permute-done.3
  390.6 4.1 collective-permute-done.2
  394.7 0.2 maximum_convert_fusion.1
  395.0 1.0 copy.76
  396.0 0.6 gather_fusion.1
  396.6 0.9 fusion.2
  397.5 0.6 fusion.6
  398.1 0.0 copy-start.2
  398.1 0.1 dynamic-slice_add_fusion
  398.2 0.6 dynamic_update_slice.7
  398.8 258.3 %all-reduce.3 = bf16[8,36,448]{2,0,1:T(8,128)(2,1)S(1)} all-reduce(f32[8,36,448]{2,0,1:T(8,128)S(1)} %dynamic_update_slice.7), channel_id=1, replica_groups=mesh['buoy'=4,'dom'=64] {'dom'}, use_global_device_ids=true, to_apply=%region_1.3 | all-reduce | flops 129024 | bytes 774144 | tf_op jit(solution)/shard_map/psum | solution.py:58
  657.1 0.3 fusion.14
  657.4 0.1 copy.79
  657.5 0.6 copy.81
  658.1 0.1 reshape.26
  658.2 0.0 copy-done.2
  658.2 0.2 convolution_convert_fusion
  658.5 0.6 copy.82
  (6 shorter events, 0.1 us)
Async XLA Ops:
  0.6 71.8 %copy-start = (bf16[2,448,448]{2,1,0:T(8,128)(2,1)S(1)}, bf16[2,448,448]{2,1,0:T(8,128)(2,1)}, u32[]{:S(2)}) copy-start(bf16[2,448,448]{2,1,0:T(8,128)(2,1)} %param.12) | copy-start | bytes 2408452
  0.6 59.5 %copy-start.6 = (s32[2]{0:T(128)S(1)}, s32[2]{0:T(128)}, u32[]{:S(2)}) copy-start(s32[2]{0:T(128)} %param.14) | copy-start | bytes 28
  0.7 59.5 %copy-start.4 = (s32[2]{0:T(128)S(1)}, s32[2]{0:T(128)}, u32[]{:S(2)}) copy-start(s32[2]{0:T(128)} %param.13) | copy-start | bytes 28
  0.7 59.6 %copy-start.3 = (f32[8,36,7]{1,0,2:T(8,128)S(1)}, f32[8,36,7]{1,0,2:T(8,128)}, u32[]{:S(2)}) copy-start(f32[8,36,7]{1,0,2:T(8,128)} %param.10) | copy-start | bytes 24196
  0.7 59.7 %copy-start.7 = (s32[2]{0:T(128)S(1)}, s32[2]{0:T(128)}, u32[]{:S(2)}) copy-start(s32[2]{0:T(128)} %param.15) | copy-start | bytes 28
  56.1 10.2 %collective-permute-start.1 = (bf16[8,36,448]{2,1,0:T(8,128)(2,1)S(1)}, bf16[8,36,448]{2,1,0:T(8,128)(2,1)S(1)}, u32[]{:S(2)}, u32[]{:S(2)}) collective-permute-start(bf16[8,36,448]{2,1,0:T(8,128)(2,1)S(1)} %copy.70), channel_id=1, source_target_pairs={{64,0},{128,64},{192,128},{65,1},{129,65},{193,129},{66,2},{130,66... | collective-permute-start | bytes 774152 | tf_op jit(solution)/shard_map/ppermute | solution.py:17
  58.9 11.7 %collective-permute-start = (bf16[8,36,448]{2,1,0:T(8,128)(2,1)S(1)}, bf16[8,36,448]{2,1,0:T(8,128)(2,1)}, u32[]{:S(2)}, u32[]{:S(2)}) collective-permute-start(bf16[8,36,448]{2,1,0:T(8,128)(2,1)S(1)} %copy.70), channel_id=1, source_target_pairs={{0,64},{64,128},{128,192},{1,65},{65,129},{129,193},{2,66},{66,130... | collective-permute-start | bytes 774152 | tf_op jit(solution)/shard_map/ppermute | solution.py:14
  66.3 0.7 copy-start.1
  72.4 260.5 %copy-start.5 = (bf16[7,448]{1,0:T(8,128)(2,1)S(1)}, bf16[7,448]{1,0:T(8,128)(2,1)}, u32[]{:S(2)}) copy-start(bf16[7,448]{1,0:T(8,128)(2,1)} %param.16) | copy-start | bytes 18820
  381.4 9.2 %collective-permute-start.3 = (bf16[8,36,448]{2,0,1:T(8,128)(2,1)S(1)}, bf16[8,36,448]{2,0,1:T(8,128)(2,1)S(1)}, u32[]{:S(2)}, u32[]{:S(2)}) collective-permute-start(bf16[8,36,448]{2,0,1:T(8,128)(2,1)S(1)} %copy.75), channel_id=1, source_target_pairs={{64,0},{128,64},{192,128},{65,1},{129,65},{193,129},{66,2},{130,66... | collective-permute-start | bytes 774152 | tf_op jit(solution)/shard_map/ppermute | solution.py:17
  383.9 10.9 %collective-permute-start.2 = (bf16[8,36,448]{2,0,1:T(8,128)(2,1)S(1)}, bf16[8,36,448]{2,0,1:T(8,128)(2,1)S(1)}, u32[]{:S(2)}, u32[]{:S(2)}) collective-permute-start(bf16[8,36,448]{2,0,1:T(8,128)(2,1)S(1)} %copy.75), channel_id=1, source_target_pairs={{0,64},{64,128},{128,192},{1,65},{65,129},{129,193},{2,66},{66,130... | collective-permute-start | bytes 774152 | tf_op jit(solution)/shard_map/ppermute | solution.py:14
  398.1 260.2 %copy-start.2 = (bf16[128,448]{0,1:T(8,128)(2,1)S(1)}, bf16[128,448]{0,1:T(8,128)(2,1)}, u32[]{:S(2)}) copy-start(bf16[128,448]{0,1:T(8,128)(2,1)} %param.17) | copy-start | bytes 344068
where the time goes:
time: 659 us
  blocking collectives  618 us (94%)
  waiting for transfers between devices  18.8 us (3%)
  starting transfers between devices  7.95 us (1%)
  local copies, waits for them, and re-layouts  7.34 us (1%)
    psum x2, blocking collectives, shards(): incident = lax.psum(partial_value, 'dom')  517 us
    all_gather x2, blocking collectives, shards(): whole = lax.all_gather(coeffs, 'dom', axis=2, tiled=True)  101 us
  transfers between devices with their start and end apart: 4, of which 4 were waited for; matrix products, arithmetic and copies ran while one was open for 0% of the time, Pallas kernels for 0%

commit v1 on v0

--- a/solution.py
+++ b/solution.py
@@ -42,7 +42,9 @@
     coeffs = initial_out
     incident_bf = None
     for step in range(ITERS):
-        whole = lax.all_gather(coeffs, "dom", axis=2, tiled=True)
+        whole = jnp.concatenate(
+            lax.all_to_all(jnp.stack([coeffs] * lax.axis_size("dom")), "dom", 0, 0), axis=2
+        )
         extended = extended_2(whole.astype(jnp.bfloat16), (("buoy", 0),), per_dev).astype(
             whole.dtype
         )

time: 659 us -> 602 us (0.914)
  blocking collectives: 618 us -> 531 us
  waiting for transfers between devices: 18.8 us -> 32.3 us
  starting transfers between devices: 7.95 us -> 20.1 us
    all_gather x2 -> x0, blocking collectives: 101 us -> none  [shards(): whole = lax.all_gather(coeffs, 'dom', axis=2, tiled=True)]
    all_to_all x0 -> x1, blocking collectives: none -> 16.7 us  [shards(): lax.all_to_all(jnp.stack([coeffs] * lax.axis_size('dom')), 'dom', 0, 0)]
    all_to_all x0 -> x1, waiting for transfers between devices: none -> 12.9 us  [shards(): lax.all_to_all(jnp.stack([coeffs] * lax.axis_size('dom')), 'dom', 0, 0)]
    all_to_all x0 -> x1, starting transfers between devices: none -> 12.1 us  [shards(): lax.all_to_all(jnp.stack([coeffs] * lax.axis_size('dom')), 'dom', 0, 0)]
  transfers between devices with their start and end apart: 4 -> 5, of which waited for: 4 -> 5; matrix products, arithmetic and copies ran while one was open for 0% -> 0% of each run, Pallas kernels for 0% -> 0%
where the time goes in v1:
time: 602 us; the launch traced here: 601 us
  blocking collectives  531 us (88%)
  waiting for transfers between devices  32.3 us (5%)
  starting transfers between devices  20.1 us (3%)
  local copies, waits for them, and re-layouts  11.4 us (2%)
    psum x2, blocking collectives, shards(): incident = lax.psum(partial_value, 'dom')  514 us
    all_to_all x1, blocking collectives, shards(): lax.all_to_all(jnp.stack([coeffs] * lax.axis_size('dom')), 'dom', 0, 0)  16.7 us
    all_to_all x1, waiting for transfers between devices, shards(): lax.all_to_all(jnp.stack([coeffs] * lax.axis_size('dom')), 'dom', 0, 0)  12.9 us
    all_to_all x1, starting transfers between devices, shards(): lax.all_to_all(jnp.stack([coeffs] * lax.axis_size('dom')), 'dom', 0, 0)  12.1 us
  transfers between devices with their start and end apart: 5, of which 5 were waited for; matrix products, arithmetic and copies ran while one was open for 0% of the time, Pallas kernels for 0%

profile of v1, /device:TPU:6, one launch (start us, length us, event | category | flops | bytes accessed | tf_op | source)
XLA Modules:
  0.0 601.2 jit_solution(17534069284994556316)
XLA Ops:
  0.6 0.0 copy-start
  0.6 0.0 copy-start.6
  0.7 0.0 copy-start.4
  0.7 0.9 broadcast_bitcast_fusion.1
  1.6 0.0 copy-start.3
  1.6 0.0 copy-start.7
  1.6 1.5 reshape.64
  3.1 12.1 %all-to-all-start = ((bf16[64,2,1008]{2,1,0:T(2,128)(2,1)}), bf16[64,2,1008]{2,1,0:T(2,128)(2,1)S(1)}, u32[]{:S(2)}, u32[]{:S(2)}) async-start(bf16[64,2,1008]{2,1,0:T(2,128)(2,1)} %reshape.64), calls=%async_computation | async-start | bytes 524288 | tf_op jit(solution)/shard_map/all_to_all | solution.py:46
  15.2 0.0 copy-done.6
  15.3 0.0 copy-done.4
  15.3 12.9 %all-to-all-done = bf16[64,2,1008]{2,1,0:T(2,128)(2,1)S(1)} async-done(((bf16[64,2,1008]{2,1,0:T(2,128)(2,1)}), bf16[64,2,1008]{2,1,0:T(2,128)(2,1)S(1)}, u32[]{:S(2)}, u32[]{:S(2)}) %all-to-all-start) | async-done | bytes 258080 | tf_op jit(solution)/shard_map/all_to_all | solution.py:46
  28.2 1.0 reshape.65
  29.2 0.7 copy.26
  29.9 2.7 collective-permute-start.1
  32.6 1.3 collective-permute-start
  34.0 0.0 copy-done.3
  34.0 0.2 copy.30
  34.1 0.0 copy-done.7
  34.2 5.8 collective-permute-done.1
  40.0 0.0 copy-start.1
  40.0 0.7 copy-done.1
  40.7 3.5 collective-permute-done
  44.2 1.3 maximum_convert_fusion
  45.5 0.0 copy-start.5
  45.5 0.6 gather_fusion
  46.1 0.0 copy-done
  46.1 0.9 fusion.4
  47.0 0.6 fusion.8
  47.6 0.1 dynamic-slice_add_fusion.1
  47.7 0.6 dynamic_update_slice.6
  48.3 257.1 %all-reduce.2 = bf16[8,36,448]{2,0,1:T(8,128)(2,1)S(1)} all-reduce(f32[8,36,448]{2,0,1:T(8,128)S(1)} %dynamic_update_slice.6), channel_id=1, replica_groups=mesh['buoy'=4,'dom'=64] {'dom'}, use_global_device_ids=true, to_apply=%region_0.0 | all-reduce | flops 129024 | bytes 774144 | tf_op jit(solution)/shard_map/psum | solution.py:60
  305.4 0.0 copy-done.5
  305.4 0.3 fusion
  305.7 0.1 broadcast_bitcast_fusion
  305.9 0.8 reshape.66
  306.7 16.7 %all_to_all.10 = bf16[64,2,1008]{2,1,0:T(2,128)(2,1)S(1)} all-to-all(bf16[64,2,1008]{2,1,0:T(2,128)(2,1)S(1)} %reshape.66), channel_id=1, replica_groups=mesh['buoy'=4,'dom'=64] {'dom'}, dimensions={0} | all-to-all | bytes 516096 | tf_op jit(solution)/shard_map/all_to_all | solution.py:46
  323.4 1.0 reshape.67
  324.4 0.7 copy.33
  325.1 2.5 collective-permute-start.3
  327.6 1.5 collective-permute-start.2
  329.0 5.9 collective-permute-done.3
  334.9 4.1 collective-permute-done.2
  339.0 0.2 maximum_convert_fusion.1
  339.2 0.6 gather_fusion.1
  339.8 0.9 fusion.2
  340.7 0.0 copy-start.2
  340.7 0.6 fusion.6
  341.3 0.1 dynamic-slice_add_fusion
  341.4 0.6 dynamic_update_slice.7
  342.0 257.1 %all-reduce.3 = bf16[8,36,448]{2,0,1:T(8,128)(2,1)S(1)} all-reduce(f32[8,36,448]{2,0,1:T(8,128)S(1)} %dynamic_update_slice.7), channel_id=1, replica_groups=mesh['buoy'=4,'dom'=64] {'dom'}, use_global_device_ids=true, to_apply=%region_1.3 | all-reduce | flops 129024 | bytes 774144 | tf_op jit(solution)/shard_map/psum | solution.py:60
  599.1 0.3 fusion.14
  599.4 0.1 copy.38
  599.5 0.6 copy.40
  600.2 0.1 reshape.38
  600.3 0.0 copy-done.2
  600.3 0.2 convolution_convert_fusion
  600.5 0.6 copy.41
  (6 shorter events, 0.1 us)
Async XLA Ops:
  0.6 45.5 %copy-start = (bf16[2,448,448]{2,1,0:T(8,128)(2,1)S(1)}, bf16[2,448,448]{2,1,0:T(8,128)(2,1)}, u32[]{:S(2)}) copy-start(bf16[2,448,448]{2,1,0:T(8,128)(2,1)} %param.12) | copy-start | bytes 2408452
  0.6 14.6 %copy-start.6 = (s32[2]{0:T(128)S(1)}, s32[2]{0:T(128)}, u32[]{:S(2)}) copy-start(s32[2]{0:T(128)} %param.14) | copy-start | bytes 28
  0.7 14.6 %copy-start.4 = (s32[2]{0:T(128)S(1)}, s32[2]{0:T(128)}, u32[]{:S(2)}) copy-start(s32[2]{0:T(128)} %param.13) | copy-start | bytes 28
  1.6 32.4 %copy-start.3 = (f32[8,36,7]{1,0,2:T(8,128)S(1)}, f32[8,36,7]{1,0,2:T(8,128)}, u32[]{:S(2)}) copy-start(f32[8,36,7]{1,0,2:T(8,128)} %param.10) | copy-start | bytes 24196
  1.6 32.5 %copy-start.7 = (s32[2]{0:T(128)S(1)}, s32[2]{0:T(128)}, u32[]{:S(2)}) copy-start(s32[2]{0:T(128)} %param.15) | copy-start | bytes 28
  3.1 25.1 %all-to-all-start = ((bf16[64,2,1008]{2,1,0:T(2,128)(2,1)}), bf16[64,2,1008]{2,1,0:T(2,128)(2,1)S(1)}, u32[]{:S(2)}, u32[]{:S(2)}) async-start(bf16[64,2,1008]{2,1,0:T(2,128)(2,1)} %reshape.64), calls=%async_computation | async-start | bytes 524288 | tf_op jit(solution)/shard_map/all_to_all | solution.py:46
  29.9 10.1 %collective-permute-start.1 = (bf16[8,36,448]{2,1,0:T(8,128)(2,1)S(1)}, bf16[8,36,448]{2,1,0:T(8,128)(2,1)S(1)}, u32[]{:S(2)}, u32[]{:S(2)}) collective-permute-start(bf16[8,36,448]{2,1,0:T(8,128)(2,1)S(1)} %copy.26), channel_id=1, source_target_pairs={{64,0},{128,64},{192,128},{65,1},{129,65},{193,129},{66,2},{130,66... | collective-permute-start | bytes 774152 | tf_op jit(solution)/shard_map/ppermute | solution.py:17
  32.6 11.6 %collective-permute-start = (bf16[8,36,448]{2,1,0:T(8,128)(2,1)S(1)}, bf16[8,36,448]{2,1,0:T(8,128)(2,1)}, u32[]{:S(2)}, u32[]{:S(2)}) collective-permute-start(bf16[8,36,448]{2,1,0:T(8,128)(2,1)S(1)} %copy.26), channel_id=1, source_target_pairs={{0,64},{64,128},{128,192},{1,65},{65,129},{129,193},{2,66},{66,130... | collective-permute-start | bytes 774152 | tf_op jit(solution)/shard_map/ppermute | solution.py:14
  40.0 0.7 copy-start.1
  45.5 259.9 %copy-start.5 = (bf16[7,448]{1,0:T(8,128)(2,1)S(1)}, bf16[7,448]{1,0:T(8,128)(2,1)}, u32[]{:S(2)}) copy-start(bf16[7,448]{1,0:T(8,128)(2,1)} %param.16) | copy-start | bytes 18820
  325.1 9.8 %collective-permute-start.3 = (bf16[8,36,448]{2,1,0:T(8,128)(2,1)S(1)}, bf16[8,36,448]{2,1,0:T(8,128)(2,1)S(1)}, u32[]{:S(2)}, u32[]{:S(2)}) collective-permute-start(bf16[8,36,448]{2,1,0:T(8,128)(2,1)S(1)} %copy.33), channel_id=1, source_target_pairs={{64,0},{128,64},{192,128},{65,1},{129,65},{193,129},{66,2},{130,66... | collective-permute-start | bytes 774152 | tf_op jit(solution)/shard_map/ppermute | solution.py:17
  327.6 11.5 %collective-permute-start.2 = (bf16[8,36,448]{2,1,0:T(8,128)(2,1)S(1)}, bf16[8,36,448]{2,1,0:T(8,128)(2,1)S(1)}, u32[]{:S(2)}, u32[]{:S(2)}) collective-permute-start(bf16[8,36,448]{2,1,0:T(8,128)(2,1)S(1)} %copy.33), channel_id=1, source_target_pairs={{0,64},{64,128},{128,192},{1,65},{65,129},{129,193},{2,66},{66,130... | collective-permute-start | bytes 774152 | tf_op jit(solution)/shard_map/ppermute | solution.py:14
  340.7 259.5 %copy-start.2 = (bf16[128,448]{0,1:T(8,128)(2,1)S(1)}, bf16[128,448]{0,1:T(8,128)(2,1)}, u32[]{:S(2)}) copy-start(bf16[128,448]{0,1:T(8,128)(2,1)} %param.17) | copy-start | bytes 344068
